TPU v7x, 256 devices: a whole 4x4x8 slice. The times are simulated.
256 devices in a mesh: seq: 32 (over z, y), exp: 8 (over x, core).
Axes of the slice: x: 4, y: 4, z: 8, core: 2. Of those that a mesh axis runs over, the one named last changes fastest.
Arguments:
- resid_rows: bfloat16 [8, 128, 3072], P('exp', 'seq'), may hold values from -6 to 6
- query_rows: bfloat16 [8, 128, 3072], P('exp', 'seq'), may hold values from -6 to 6
- key_rows: bfloat16 [8, 4096, 3072], P('exp', 'seq'), may hold values from -6 to 6
- value_rows: bfloat16 [8, 4096, 3072], P('exp', 'seq'), may hold values from -6 to 6
- log_decay: float32 [8, 48, 4096], P('exp', None, 'seq'), may hold values from -1 to 0
- read_pos: int32 [8, 128], P('exp', 'seq'), may hold values from 0 to 4095, as said below
- expert_ids: int32 [8, 128, 2], P('exp', 'seq'), may hold values from 0 to 7, all different within a row; in each aligned block of 4 rows (0 to 3, 4 to 7, ..., all dimensions but the last counted through in order) at most 2 rows name the same one
- pair_order: int32 [8], replicated, may hold values from 0 to 7, each once
- lengths: int32 [8], replicated, may hold values from 1 to 4096
- norm_gain: bfloat16 [3072], replicated, may hold values from 0.5 to 1.5
- router_weight: bfloat16 [3072, 8], replicated, may hold values from -0.109375 to 0.109375
- score_weight: bfloat16 [3072], replicated, may hold values from -0.109375 to 0.109375
- gate_weight: bfloat16 [8, 3072, 9216], P('exp', None, 'seq'), may hold values from -0.109375 to 0.109375
- up_weight: bfloat16 [8, 3072, 9216], P('exp', None, 'seq'), may hold values from -0.109375 to 0.109375
- down_weight: bfloat16 [8, 9216, 3072], P('exp', 'seq'), may hold values from -0.0625 to 0.0625
Outputs:
- pair_loss: float32 [], replicated
- grad_query: float32 [8, 128, 3072], P('exp', 'seq')
- grad_resid: float32 [8, 128, 3072], P('exp', 'seq')
- grad_keys: bfloat16 [8, 4096, 3072], P('exp', 'seq')
- grad_values: bfloat16 [8, 4096, 3072], P('exp', 'seq')
Inputs may be any that keep to these rules, and one draw needn't show every extreme that they name: `read_pos`: each aligned block j of 4 entries of a sequence holds strictly increasing positions from j * 128 to (j + 1) * 128 - 1, the last of them being (j + 1) * 128 - 1. `expert_ids`: the two entries of a row differ; in the rows of one device (aligned blocks of 4 rows) no expert is named by more than 2 rows. `pair_order`: each sequence appears once.
All inputs are finite; a program needn't handle non-finite values.
Results may differ from a plain program's by a relative error of at most 0.018.
Values may be sent and summed in bfloat16 or wider, within the bound.
No kernel may reach another device: no remote copies, remote signals or barrier semaphores. Data moves between devices by JAX's collectives and lax.ppermute only.
A program may use at most 128 MiB of HBM per device.

v0:
```python
import jax
import jax.numpy as jnp
from jax import lax
from jax.sharding import PartitionSpec as P

PRECISE = lax.Precision.HIGHEST
EPSILON = 1e-06
LENGTH_WEIGHT = 4.0
SCORE_SCALE = 256.0


def carried_in(value, axis, join, neutral, backward):
    count = lax.axis_size(axis)
    place = lax.axis_index(axis)
    ahead = count - 1 - place if backward else place
    gathered = jax.tree.map(
        lambda a, kind: lax.all_gather(a.astype(kind), axis), value, (jnp.bfloat16, jnp.bfloat16)
    )
    state = jax.tree.map(lambda a, e: jnp.zeros_like(a) + jnp.asarray(e, a.dtype), value, neutral)

    def one(lap, state):
        source = count - 1 - lap if backward else lap
        return join(
            state,
            jax.tree.map(
                lambda a, own: lax.dynamic_index_in_dim(a, source, 0, False).astype(own.dtype),
                gathered,
                value,
            ),
        )

    return lax.fori_loop(0, ahead, one, state)


def merge_states(earlier, later):
    return (earlier[0] * later[0], later[0][:, None, None] * earlier[1] + later[1])


def chain_prefix(decay, summary, backwards):
    blank = (jnp.ones_like(decay), jnp.zeros_like(summary))
    joined = carried_in((decay, summary), "seq", merge_states, blank, backwards)
    return joined[1]


def readout_weights(cumulated, places):
    positions = jnp.arange(cumulated.shape[1], dtype=jnp.int32)
    one_hot = (places[:, None] == positions[None, :]).astype(jnp.float32)
    at_read = jnp.dot(cumulated, one_hot.T, precision=PRECISE)
    allowed = positions[None, :] <= places[:, None]
    exponent = jnp.where(allowed[None], at_read[:, :, None] - cumulated[:, None, :], -1e30)
    return (at_read, jnp.exp(exponent))


def preference_loss(rewards, pair_order, lengths, total_length):
    count = rewards.shape[0]
    ordering = (pair_order[:, None] == jnp.arange(count, dtype=jnp.int32)[None, :]).astype(
        jnp.float32
    )
    ranked = jnp.dot(ordering, rewards, precision=PRECISE).reshape(count // 2, 2)
    fitted = jnp.mean(jax.nn.softplus(ranked[:, 1] - ranked[:, 0]))
    share = lengths.astype(jnp.float32) / total_length
    scatter_breadth = jnp.mean((rewards - jnp.mean(rewards)) * (share - jnp.mean(share)))
    return fitted + LENGTH_WEIGHT * scatter_breadth * scatter_breadth


def to_experts(slots):
    return lax.all_to_all(slots, "exp", split_axis=0, concat_axis=0, tiled=True)


def over_slots(arrived, project):
    return project(lax.all_gather(arrived, "seq", axis=0, tiled=True), jnp.int32(0))


def collect(project, expert_count, capacity):
    slot_count = expert_count * capacity
    summed = lax.psum_scatter(
        project(jnp.int32(0), slot_count * lax.axis_size("seq")).astype(jnp.bfloat16),
        "seq",
        scatter_dimension=0,
        tiled=True,
    )
    shaped = summed.reshape(expert_count, capacity, -1)
    return lax.all_to_all(shaped, "exp", split_axis=0, concat_axis=0, tiled=True)


def per_device(
    resid_rows,
    query_rows,
    key_rows,
    value_rows,
    log_decay,
    read_pos,
    expert_ids,
    pair_order,
    lengths,
    norm_gain,
    router_weight,
    score_weight,
    gate_weight,
    up_weight,
    down_weight,
):
    seq_count = lax.axis_size("seq")
    exp_count = lax.axis_size("exp")
    seq_index = lax.axis_index("seq")
    exp_index = lax.axis_index("exp")
    token_count = key_rows.shape[1]
    model_width = key_rows.shape[2]
    head_count = log_decay.shape[1]
    head_size = model_width // head_count
    read_count = query_rows.shape[1]
    expert_count = router_weight.shape[1]
    capacity = max(2, 4 * read_count // exp_count)
    keys_half = key_rows[0].reshape(token_count, head_count, head_size)
    values_half = value_rows[0].reshape(token_count, head_count, head_size)
    query_half = query_rows[0].reshape(read_count, head_count, head_size)
    keys_float = keys_half.astype(jnp.float32)
    values_float = values_half.astype(jnp.float32)
    query_float = query_half.astype(jnp.float32)
    cumulated = jnp.cumsum(log_decay[0], axis=1)
    group_decay = jnp.exp(cumulated[:, -1])
    tail_decay = jnp.exp(cumulated[:, -1:] - cumulated).T[:, :, None]
    own_state = jnp.einsum("thi,thj->hij", keys_float * tail_decay, values_float, precision=PRECISE)
    state_in = chain_prefix(group_decay, own_state, False)
    places = read_pos[0] - seq_index * token_count
    at_read, weight = readout_weights(cumulated, places)
    lift = jnp.exp(at_read).T[:, :, None]
    query_key = (
        jnp.einsum("rhi,thi->hrt", query_half, keys_half, preferred_element_type=jnp.float32)
        / head_size
    )
    attended = jnp.einsum("hrt,thj->rhj", weight * query_key, values_float, precision=PRECISE)
    attended = (
        attended
        + lift * jnp.einsum("rhi,hij->rhj", query_float, state_in, precision=PRECISE) / head_size
    )
    residual = resid_rows[0].astype(jnp.float32) + attended.reshape(read_count, model_width)
    inverse = lax.rsqrt(jnp.mean(residual * residual, axis=1, keepdims=True) + EPSILON)
    unit_rows = residual * inverse
    gain_float = norm_gain.astype(jnp.float32)
    normed = (unit_rows * gain_float).astype(jnp.bfloat16)
    logits = jnp.dot(normed, router_weight, preferred_element_type=jnp.float32)
    picks = (
        expert_ids[0][:, :, None] == jnp.arange(expert_count, dtype=jnp.int32)[None, None, :]
    ).astype(jnp.float32)
    chosen = jnp.einsum("rke,re->rk", picks, logits, precision=PRECISE)
    first = jax.nn.sigmoid(chosen[:, 0] - chosen[:, 1])
    gates = jnp.stack([first, 1.0 - first], axis=1)
    flat = picks.reshape(read_count * 2, expert_count)
    earlier = jnp.cumsum(flat, axis=0) - flat
    slot_index = jnp.sum(earlier * flat, axis=1)
    slot_hot = (slot_index[:, None] == jnp.arange(capacity, dtype=jnp.float32)[None, :]).astype(
        jnp.float32
    )
    placement = (
        (flat[:, :, None] * slot_hot[:, None, :])
        .reshape(read_count * 2, expert_count * capacity)
        .astype(jnp.bfloat16)
    )
    doubled = jnp.repeat(normed, 2, axis=0)
    outgoing = jnp.dot(placement.T, doubled, preferred_element_type=jnp.float32).astype(
        jnp.bfloat16
    )
    arrived = to_experts(outgoing.reshape(expert_count, capacity, model_width)).reshape(
        expert_count * capacity, model_width
    )
    gate_w = gate_weight[0]
    up_w = up_weight[0]
    down_w = down_weight[0]
    hidden_count = gate_w.shape[1]

    def project_in(piece, start):
        gate_part = jnp.dot(piece, gate_w, preferred_element_type=jnp.float32)
        up_part = jnp.dot(piece, up_w, preferred_element_type=jnp.float32)
        return jnp.concatenate([gate_part, up_part], axis=1)

    projected = over_slots(arrived, project_in)
    pre_gate = projected[:, :hidden_count]
    pre_up = projected[:, hidden_count:]
    gate_sigmoid = jax.nn.sigmoid(pre_gate)
    activated = (pre_gate * gate_sigmoid * pre_up).astype(jnp.bfloat16)

    def project_out(start, count):
        return jnp.dot(activated, down_w, preferred_element_type=jnp.float32)

    returned = collect(project_out, expert_count, capacity)
    expert_out = jnp.dot(
        placement,
        returned.reshape(expert_count * capacity, model_width),
        preferred_element_type=jnp.float32,
    )
    expert_out = expert_out.reshape(read_count, 2, model_width)
    mixed = residual + jnp.sum(gates[:, :, None] * expert_out, axis=1)
    score_float = score_weight.astype(jnp.float32)
    score = jnp.dot(mixed, score_float, precision=PRECISE)
    own_total = jnp.sum(score) / (read_count * seq_count)
    marked = jnp.where(jnp.arange(exp_count) == exp_index, own_total, 0.0)
    rewards = lax.psum(marked, ("seq", "exp"))
    pair_loss, d_reward = jax.value_and_grad(preference_loss)(
        rewards, pair_order, lengths, token_count * seq_count
    )
    own_grad = jnp.sum(jnp.where(jnp.arange(exp_count) == exp_index, d_reward, 0.0)) * SCORE_SCALE
    d_mixed = jnp.broadcast_to((own_grad * score_float)[None, :], (read_count, model_width))
    d_out = (gates[:, :, None] * d_mixed[:, None, :]).astype(jnp.bfloat16)
    d_gates = jnp.einsum("rd,rkd->rk", d_mixed, expert_out, precision=PRECISE)
    d_logit = (d_gates[:, 0] - d_gates[:, 1]) * first * (1.0 - first)
    back_out = jnp.dot(
        placement.T, d_out.reshape(read_count * 2, model_width), preferred_element_type=jnp.float32
    ).astype(jnp.bfloat16)
    back_arrived = to_experts(back_out.reshape(expert_count, capacity, model_width)).reshape(
        expert_count * capacity, model_width
    )

    def project_back(piece, start):
        return jnp.einsum("sd,fd->sf", piece, down_w, preferred_element_type=jnp.float32)

    d_act = over_slots(back_arrived, project_back)
    d_pre_gate = (d_act * pre_up * gate_sigmoid * (1.0 + pre_gate * (1.0 - gate_sigmoid))).astype(
        jnp.bfloat16
    )
    d_pre_up = (d_act * pre_gate * gate_sigmoid).astype(jnp.bfloat16)

    def project_in_back(start, count):
        gate_term = jnp.einsum("sf,df->sd", d_pre_gate, gate_w, preferred_element_type=jnp.float32)
        up_term = jnp.einsum("sf,df->sd", d_pre_up, up_w, preferred_element_type=jnp.float32)
        return gate_term + up_term

    d_in_slots = collect(project_in_back, expert_count, capacity)
    d_in = jnp.dot(
        placement,
        d_in_slots.reshape(expert_count * capacity, model_width),
        preferred_element_type=jnp.float32,
    )
    d_in = d_in.reshape(read_count, 2, model_width)
    columns = jnp.einsum("rke,de->rkd", picks, router_weight.astype(jnp.float32), precision=PRECISE)
    d_normed = jnp.sum(d_in, axis=1) + d_logit[:, None] * (columns[:, 0] - columns[:, 1])
    d_unit = d_normed * gain_float
    grad_resid = d_mixed + inverse * (
        d_unit - unit_rows * jnp.mean(d_unit * unit_rows, axis=1, keepdims=True)
    )
    rounded = grad_resid.astype(jnp.bfloat16)
    d_half = rounded.reshape(read_count, head_count, head_size)
    d_attended = d_half.astype(jnp.float32)
    summary = (
        jnp.einsum("rhi,rhj->hij", query_float * lift, d_attended, precision=PRECISE) / head_size
    )
    suffix = chain_prefix(group_decay, summary, True)
    grad_dot = (
        jnp.einsum("rhj,thj->hrt", d_half, values_half, preferred_element_type=jnp.float32)
        / head_size
    )
    grad_query = jnp.einsum("hrt,thi->rhi", weight * grad_dot, keys_float, precision=PRECISE)
    grad_query = (
        grad_query
        + lift * jnp.einsum("rhj,hij->rhi", d_attended, state_in, precision=PRECISE) / head_size
    )
    grad_keys = jnp.einsum("hrt,rhi->thi", weight * grad_dot, query_float, precision=PRECISE)
    grad_keys = grad_keys + tail_decay * jnp.einsum(
        "hij,thj->thi", suffix, values_float, precision=PRECISE
    )
    grad_values = jnp.einsum("hrt,rhj->thj", weight * query_key, d_attended, precision=PRECISE)
    grad_values = grad_values + tail_decay * jnp.einsum(
        "thi,hij->thj", keys_float, suffix, precision=PRECISE
    )
    return (
        pair_loss,
        grad_query.reshape(1, read_count, model_width),
        grad_resid.reshape(1, read_count, model_width),
        grad_keys.reshape(1, token_count, model_width).astype(jnp.bfloat16),
        grad_values.reshape(1, token_count, model_width).astype(jnp.bfloat16),
    )


def solution(mesh):
    in_specs = (
        P("exp", "seq", None),
        P("exp", "seq", None),
        P("exp", "seq", None),
        P("exp", "seq", None),
        P("exp", None, "seq"),
        P("exp", "seq"),
        P("exp", "seq", None),
        P(),
        P(),
        P(),
        P(),
        P(),
        P("exp", None, "seq"),
        P("exp", None, "seq"),
        P("exp", "seq", None),
    )
    out_specs = (
        P(),
        P("exp", "seq", None),
        P("exp", "seq", None),
        P("exp", "seq", None),
        P("exp", "seq", None),
    )
    return jax.shard_map(
        per_device, mesh=mesh, in_specs=in_specs, out_specs=out_specs, check_vma=False
    )
```

profile of v0, /device:TPU:1, one launch (start us, length us, event | category | flops | bytes accessed | tf_op | source)
XLA Modules:
  0.0 1303.2 jit_solution(8809889284805440682)
XLA Ops:
  12.1 2.2 fusion.17
  16.3 65.9 %all-reduce.2 = bf16[1536]{0:T(1024)(128)(2,1)S(1)} all-reduce(bf16[1536]{0:T(1024)(128)(2,1)S(1)} %dynamic-update-slice), channel_id=2, replica_groups=mesh['seq'=32,'exp'=8] {'seq'}, use_global_device_ids=true, to_apply=%add.2 | all-reduce | flops 1536 | bytes 6144
  89.4 111.9 %all-gather.12.cloned.1.call-done = bf16[1536,64,64]{2,1,0:T(8,128)(2,1)} async-done(((bf16[48,64,64]{2,1,0:T(8,128)(2,1)}), bf16[1536,64,64]{2,1,0:T(8,128)(2,1)}) %all-gather.12.cloned.1.call-update) | async-done | bytes 12582928 | tf_op jit(solution)/shard_map/all_gather | solution.py:17
  212.8 10.7 all_to_all.20
  225.1 137.3 %all-gather.8.cloned.1.call-done = bf16[512,3072]{1,0:T(8,128)(2,1)} async-done(((bf16[16,3072]{1,0:T(8,128)(2,1)}), bf16[512,3072]{1,0:T(8,128)(2,1)}) %all-gather.8.cloned.1.call-update) | async-done | bytes 3145744 | tf_op jit(solution)/shard_map/all_gather | solution.py:71
  362.4 3.7 fusion.8
  368.3 3.5 convolution_convert_fusion
  382.1 207.1 %reduce-scatter.3.cloned.1.call-done = bf16[16,3072]{1,0:T(8,128)(2,1)} async-done(((bf16[512,3072]{1,0:T(8,128)(2,1)}), bf16[16,3072]{1,0:T(8,128)(2,1)}) %reduce-scatter.3.cloned.1.call-update) | async-done | bytes 98320 | tf_op jit(solution)/shard_map/reduce_scatter | solution.py:76
  590.8 10.0 all-to-all-start.1
  603.3 2.6 all-to-all-done.1
  613.3 74.1 %psum.7 = f32[8]{0:T(128)} all-reduce(f32[8]{0:T(128)} %compare_select_fusion.4), channel_id=1, replica_groups=mesh['seq'=32,'exp'=8] {'seq','exp'}, use_global_device_ids=true, to_apply=%region_9.10 | all-reduce | flops 8 | bytes 64 | tf_op jit(solution)/shard_map/psum | solution.py:198
  705.9 9.6 all_to_all.21
  717.2 72.2 %all-gather.10.cloned.1.call-done = bf16[512,3072]{1,0:T(8,128)(2,1)} async-done(((bf16[16,3072]{1,0:T(8,128)(2,1)}), bf16[512,3072]{1,0:T(8,128)(2,1)}) %all-gather.10.cloned.1.call-update) | async-done | bytes 3145744 | tf_op jit(solution)/shard_map/all_gather | solution.py:71
  789.4 3.1 fusion
  794.7 3.7 add_convert_fusion
  800.2 215.3 %reduce-scatter.5.cloned.1.call-done = bf16[16,3072]{1,0:T(8,128)(2,1)} async-done(((bf16[512,3072]{1,0:T(8,128)(2,1)}), bf16[16,3072]{1,0:T(8,128)(2,1)}) %reduce-scatter.5.cloned.1.call-update) | async-done | bytes 98320 | tf_op jit(solution)/shard_map/reduce_scatter | solution.py:76
  1017.2 10.0 all-to-all-start.3
  1027.3 4.9 all-to-all-done.3
  1033.6 3.2 multiply_convert_fusion
  1049.3 167.0 %all-gather.14.cloned.1.call-done = bf16[1536,64,64]{2,1,0:T(8,128)(2,1)} async-done(((bf16[48,64,64]{2,1,0:T(8,128)(2,1)}), bf16[1536,64,64]{2,1,0:T(8,128)(2,1)}) %all-gather.14.cloned.1.call-update) | async-done | bytes 12582928 | tf_op jit(solution)/shard_map/all_gather | solution.py:17
  1216.5 68.8 %while.27 = (s32[]{:T(128)}, f32[48,64,64]{2,1,0:T(8,128)S(1)}, s32[]{:T(128)}, bf16[32,48]{1,0:T(8,128)(2,1)}, bf16[32,48,64,64]{3,2,1,0:T(8,128)(2,1)}, /*index=5*/s32[]{:T(128)}, s32[]{:T(128)}, s32[]{:T(128)}, s32[]{:T(128)}) while((s32[]{:T(128)}, f32[48,64,64]{2,1,0:T(8,128)S(1)}, s32[]{:T(128)}, bf16[32,48]{1,0:T(8,128)(2,1)}, ...), condition=%wide.region_20.21_spmd, body=%wide.region_19.20_spmd.sunk | while | flops 589878 | bytes 1966715 | solution.py:32
  1285.3 2.4 fusion.13
  1288.9 4.1 fusion.11
  1293.0 2.3 copy.78
  (278 shorter events, 152.6 us)
Async XLA Ops:
  7.2 361.1 %copy-start = (bf16[1,288,3072]{2,1,0:T(8,128)(2,1)S(1)}, bf16[1,288,3072]{2,1,0:T(8,128)(2,1)}, u32[]{:S(2)}) copy-start(bf16[1,288,3072]{2,1,0:T(8,128)(2,1)} %param.33) | copy-start | bytes 5308420
  7.2 194.1 %all-gather.12.cloned.1.call-start = ((), (), s32[]{:S(2)}) async-start(), calls=%async_computation.10 | async-start | bytes 25952256 | tf_op jit(solution)/shard_map/all_gather | solution.py:17
  8.4 77.3 %copy-start.24 = (f32[48,128]{1,0:T(8,128)}, f32[48,128]{1,0:T(8,128)S(1)}, u32[]{:S(2)}) copy-start(f32[48,128]{1,0:T(8,128)S(1)} %reduce_window_sum.22) | copy-start | bytes 73732
  10.2 75.5 %copy-start.2 = (bf16[1,128,3072]{1,2,0:T(8,128)(2,1)}, bf16[1,128,3072]{1,2,0:T(8,128)(2,1)S(1)}, u32[]{:S(2)}) copy-start(bf16[1,128,3072]{1,2,0:T(8,128)(2,1)S(1)} %copy.58) | copy-start | bytes 2359300
  12.0 74.8 %copy-start.4 = (bf16[1,128,3072]{1,2,0:T(8,128)(2,1)}, bf16[1,128,3072]{1,2,0:T(8,128)(2,1)S(1)}, u32[]{:S(2)}) copy-start(bf16[1,128,3072]{1,2,0:T(8,128)(2,1)S(1)} %copy.60) | copy-start | bytes 2359300
  12.0 70.9 %copy-start.49 = (s32[1,4]{1,0:T(1,128)S(1)}, s32[1,4]{1,0:T(1,128)}, u32[]{:S(2)}) copy-start(s32[1,4]{1,0:T(1,128)} %param.24) | copy-start | bytes 52
  12.1 72.5 %copy-start.36 = (bf16[1,4,3072]{2,1,0:T(4,128)(2,1)S(1)}, bf16[1,4,3072]{2,1,0:T(4,128)(2,1)}, u32[]{:S(2)}) copy-start(bf16[1,4,3072]{2,1,0:T(4,128)(2,1)} %param.20) | copy-start | bytes 73732
  12.1 72.6 %copy-start.25 = (bf16[1,4,3072]{2,1,0:T(4,128)(2,1)S(1)}, bf16[1,4,3072]{2,1,0:T(4,128)(2,1)}, u32[]{:S(2)}) copy-start(bf16[1,4,3072]{2,1,0:T(4,128)(2,1)} %param.19) | copy-start | bytes 73732
  14.3 348.1 %all-gather.8.cloned.1.call-start = ((), (), s32[]{:S(2)}) async-start(), calls=%async_computation.6 | async-start | bytes 3244032 | tf_op jit(solution)/shard_map/all_gather | solution.py:71
  84.6 116.8 %copy-start.12 = (bf16[4,48,64]{2,1,0:T(8,128)(2,1)}, bf16[4,48,64]{2,1,0:T(8,128)(2,1)S(1)}, u32[]{:S(2)}) copy-start(bf16[4,48,64]{2,1,0:T(8,128)(2,1)S(1)} %reshape_squeeze.9) | copy-start | bytes 73732
  85.7 115.8 %copy-start.52 = (pred[4,128]{1,0:T(4,128)(4,1)}, pred[4,128]{1,0:T(4,128)(4,1)S(1)}, u32[]{:S(2)}) copy-start(pred[4,128]{1,0:T(4,128)(4,1)S(1)} %iota_compare_fusion.6) | copy-start | bytes 1540
  225.1 364.1 %reduce-scatter.3.cloned.1.call-start = ((), (), s32[]{:S(2)}) async-start(), calls=%async_computation.7 | async-start | bytes 3244032 | tf_op jit(solution)/shard_map/reduce_scatter | solution.py:76
  590.8 15.1 %all-to-all-start.1 = ((bf16[8,2,3072]{2,1,0:T(2,128)(2,1)}), bf16[8,2,3072]{2,1,0:T(2,128)(2,1)}, u32[]{:S(2)}, u32[]{:S(2)}) async-start(bf16[8,2,3072]{2,1,0:T(2,128)(2,1)} %reshape.392), calls=%async_computation.2 | async-start | bytes 196608 | tf_op jit(solution)/shard_map/all_to_all | solution.py:83
  600.8 188.6 %all-gather.10.cloned.1.call-start = ((), (), s32[]{:S(2)}) async-start(), calls=%async_computation.8 | async-start | bytes 3244032 | tf_op jit(solution)/shard_map/all_gather | solution.py:71
  717.1 298.5 %reduce-scatter.5.cloned.1.call-start = ((), (), s32[]{:S(2)}) async-start(), calls=%async_computation.9 | async-start | bytes 3244032 | tf_op jit(solution)/shard_map/reduce_scatter | solution.py:76
  798.3 228.8 %copy-start.45 = (f32[4,1]{0,1:T(1,128)S(1)}, f32[4,1]{0,1:T(1,128)}, u32[]{:S(2)}) copy-start(f32[4,1]{0,1:T(1,128)} %get-tuple-element.175) | copy-start | bytes 52
  798.4 233.9 %copy-start.39 = (bf16[4,2,16]{2,0,1:T(4,128)(2,1)S(1)}, bf16[4,2,16]{2,0,1:T(4,128)(2,1)}, u32[]{:S(2)}) copy-start(bf16[4,2,16]{2,0,1:T(4,128)(2,1)} %copy.67) | copy-start | bytes 772
  798.4 234.1 %copy-start.18 = (f32[4,3072]{1,0:T(4,128)S(1)}, f32[4,3072]{1,0:T(4,128)}, u32[]{:S(2)}) copy-start(f32[4,3072]{1,0:T(4,128)} %reshape.388) | copy-start | bytes 147460
  798.4 234.1 %copy-start.26 = (bf16[1,4,3072]{2,1,0:T(4,128)(2,1)S(1)}, bf16[1,4,3072]{2,1,0:T(4,128)(2,1)}, u32[]{:S(2)}) copy-start(bf16[1,4,3072]{2,1,0:T(4,128)(2,1)} %param.19) | copy-start | bytes 73732
  798.4 234.1 %copy-start.42 = (f32[4]{0:T(128)S(1)}, f32[4]{0:T(128)}, u32[]{:S(2)}) copy-start(f32[4]{0:T(128)} %add_rsqrt_fusion) | copy-start | bytes 52
  799.0 234.5 %copy-start.13 = (bf16[4,48,64]{2,1,0:T(8,128)(2,1)S(1)}, bf16[4,48,64]{2,1,0:T(8,128)(2,1)}, u32[]{:S(2)}) copy-start(bf16[4,48,64]{2,1,0:T(8,128)(2,1)} %copy-done.12) | copy-start | bytes 73732
  1017.2 15.0 %all-to-all-start.3 = ((bf16[8,2,3072]{2,1,0:T(2,128)(2,1)}), bf16[8,2,3072]{2,1,0:T(2,128)(2,1)S(1)}, u32[]{:S(2)}, u32[]{:S(2)}) async-start(bf16[8,2,3072]{2,1,0:T(2,128)(2,1)} %reshape.398), calls=%async_computation.5 | async-start | bytes 196608 | tf_op jit(solution)/shard_map/all_to_all | solution.py:83
  1027.2 189.1 %all-gather.14.cloned.1.call-start = ((), (), s32[]{:S(2)}) async-start(), calls=%async_computation.11 | async-start | bytes 25952256 | tf_op jit(solution)/shard_map/all_gather | solution.py:17
  1216.5 68.8 %copy-start.22 = (f32[128,48]{0,1:T(8,128)S(1)}, f32[128,48]{0,1:T(8,128)}, u32[]{:S(2)}) copy-start(f32[128,48]{0,1:T(8,128)} %copy-done.21) | copy-start | bytes 73732
  (37 other events, 111.9 us)
Sparse Core Ops, SparseCore 0:
  14.5 186.7 all-gather.11
  225.2 137.1 all-gather.7
  371.9 217.2 reduce-scatter.2
  717.3 72.1 all-gather.9
  798.5 216.9 reduce-scatter.4
  1036.9 179.3 all-gather.13
where the time goes:
time: 1310 us; the launch traced here: 1300 us
  waiting for transfers between devices  918 us (70%)
  blocking collectives  160 us (12%)
  other arithmetic  85.5 us (7%)
  matrix products  54 us (4%)
  local copies, waits for them, and re-layouts  41.1 us (3%)
  between operations  22.6 us (2%)
  starting transfers between devices  20.2 us (2%)
    reduce_scatter x2, waiting for transfers between devices, collect(): lax.psum_scatter(project(jnp.int32(0), slot_count * lax.axis_size('seq'))...  422 us
    all_gather x2, waiting for transfers between devices, carried_in(): lax.all_gather(a.astype(kind), axis)  279 us
    all_gather x2, waiting for transfers between devices, over_slots(): lax.all_gather(arrived, 'seq', axis=0, tiled=True)  210 us
    psum x1, blocking collectives, per_device(): rewards = lax.psum(marked, ('seq', 'exp'))  74.1 us
    unnamed x1, blocking collectives  65.9 us
    add x31, other arithmetic, merge_states(): later[0][:, None, None] * earlier[1] + later[1]  46.5 us
  transfers between devices with their start and end apart: 8, of which 8 were waited for; matrix products, arithmetic and copies ran while one was open for 2% of the time, Pallas kernels for 0%

commit v1 on v0

--- a/solution.py
+++ b/solution.py
@@ -195,7 +195,7 @@
     score = jnp.dot(mixed, score_float, precision=PRECISE)
     own_total = jnp.sum(score) / (read_count * seq_count)
     marked = jnp.where(jnp.arange(exp_count) == exp_index, own_total, 0.0)
-    rewards = lax.psum(marked, ("seq", "exp"))
+    rewards = lax.psum(lax.psum(marked, "seq"), "exp")
     pair_loss, d_reward = jax.value_and_grad(preference_loss)(
         rewards, pair_order, lengths, token_count * seq_count
     )

time: 1310 us -> 1320 us (level)
    psum x1 -> x2, blocking collectives: 74.1 us -> 85.9 us  [per_device(): rewards = lax.psum(lax.psum(marked, 'seq'), 'exp')]
where the time goes in v1:
time: 1320 us
  waiting for transfers between devices  919 us (70%)
  blocking collectives  172 us (13%)
  other arithmetic  85.9 us (7%)
  matrix products  54.1 us (4%)
  local copies, waits for them, and re-layouts  41.5 us (3%)
  between operations  22.9 us (2%)
  starting transfers between devices  20.2 us (2%)
    reduce_scatter x2, waiting for transfers between devices, collect(): lax.psum_scatter(project(jnp.int32(0), slot_count * lax.axis_size('seq'))...  423 us
    all_gather x2, waiting for transfers between devices, carried_in(): lax.all_gather(a.astype(kind), axis)  279 us
    all_gather x2, waiting for transfers between devices, over_slots(): lax.all_gather(arrived, 'seq', axis=0, tiled=True)  209 us
    psum x2, blocking collectives, per_device(): rewards = lax.psum(lax.psum(marked, 'seq'), 'exp')  85.9 us
    unnamed x1, blocking collectives  65.9 us
    add x31, other arithmetic, merge_states(): later[0][:, None, None] * earlier[1] + later[1]  46.5 us
  transfers between devices with their start and end apart: 8, of which 8 were waited for; matrix products, arithmetic and copies ran while one was open for 2% of the time, Pallas kernels for 0%

profile of v1, /device:TPU:1, one launch (start us, length us, event | category | flops | bytes accessed | tf_op | source)
XLA Modules:
  0.0 1316.6 jit_solution(13590087046404356695)
XLA Ops:
  16.3 65.9 %all-reduce.2 = bf16[1536]{0:T(1024)(128)(2,1)S(1)} all-reduce(bf16[1536]{0:T(1024)(128)(2,1)S(1)} %dynamic-update-slice), channel_id=2, replica_groups=mesh['seq'=32,'exp'=8] {'seq'}, use_global_device_ids=true, to_apply=%add.2 | all-reduce | flops 1536 | bytes 6144
  89.4 111.9 %all-gather.12.cloned.1.call-done = bf16[1536,64,64]{2,1,0:T(8,128)(2,1)} async-done(((bf16[48,64,64]{2,1,0:T(8,128)(2,1)}), bf16[1536,64,64]{2,1,0:T(8,128)(2,1)}) %all-gather.12.cloned.1.call-update) | async-done | bytes 12582928 | tf_op jit(solution)/shard_map/all_gather | solution.py:17
  212.9 10.7 all_to_all.20
  225.2 137.3 %all-gather.8.cloned.1.call-done = bf16[512,3072]{1,0:T(8,128)(2,1)} async-done(((bf16[16,3072]{1,0:T(8,128)(2,1)}), bf16[512,3072]{1,0:T(8,128)(2,1)}) %all-gather.8.cloned.1.call-update) | async-done | bytes 3145744 | tf_op jit(solution)/shard_map/all_gather | solution.py:71
  362.5 3.7 fusion.8
  368.4 3.6 convolution_convert_fusion
  382.5 207.0 %reduce-scatter.3.cloned.1.call-done = bf16[16,3072]{1,0:T(8,128)(2,1)} async-done(((bf16[512,3072]{1,0:T(8,128)(2,1)}), bf16[16,3072]{1,0:T(8,128)(2,1)}) %reduce-scatter.3.cloned.1.call-update) | async-done | bytes 98320 | tf_op jit(solution)/shard_map/reduce_scatter | solution.py:76
  591.1 9.7 all-to-all-start.1
  602.1 3.8 all-to-all-done.1
  613.3 58.7 %psum.14 = f32[8]{0:T(128)} all-reduce(f32[8]{0:T(128)} %compare_select_fusion.4), channel_id=1, replica_groups=mesh['seq'=32,'exp'=8] {'seq'}, use_global_device_ids=true, to_apply=%region_9.10 | all-reduce | flops 8 | bytes 64 | tf_op jit(solution)/shard_map/psum | solution.py:198
  673.3 27.2 %psum.15 = f32[8]{0:T(128)} all-reduce(f32[8]{0:T(128)} %psum.14), channel_id=1, replica_groups=mesh['seq'=32,'exp'=8] {'exp'}, use_global_device_ids=true, to_apply=%region_10.11 | all-reduce | flops 8 | bytes 64 | tf_op jit(solution)/shard_map/psum | solution.py:198
  719.7 9.6 all_to_all.21
  731.1 71.3 %all-gather.10.cloned.1.call-done = bf16[512,3072]{1,0:T(8,128)(2,1)} async-done(((bf16[16,3072]{1,0:T(8,128)(2,1)}), bf16[512,3072]{1,0:T(8,128)(2,1)}) %all-gather.10.cloned.1.call-update) | async-done | bytes 3145744 | tf_op jit(solution)/shard_map/all_gather | solution.py:71
  802.5 3.1 fusion
  807.7 3.7 add_convert_fusion
  813.3 215.6 %reduce-scatter.5.cloned.1.call-done = bf16[16,3072]{1,0:T(8,128)(2,1)} async-done(((bf16[512,3072]{1,0:T(8,128)(2,1)}), bf16[16,3072]{1,0:T(8,128)(2,1)}) %reduce-scatter.5.cloned.1.call-update) | async-done | bytes 98320 | tf_op jit(solution)/shard_map/reduce_scatter | solution.py:76
  1030.5 10.2 all-to-all-start.3
  1040.7 4.9 all-to-all-done.3
  1047.0 3.2 multiply_convert_fusion
  1062.8 166.8 %all-gather.14.cloned.1.call-done = bf16[1536,64,64]{2,1,0:T(8,128)(2,1)} async-done(((bf16[48,64,64]{2,1,0:T(8,128)(2,1)}), bf16[1536,64,64]{2,1,0:T(8,128)(2,1)}) %all-gather.14.cloned.1.call-update) | async-done | bytes 12582928 | tf_op jit(solution)/shard_map/all_gather | solution.py:17
  1229.8 68.8 %while.27 = (s32[]{:T(128)}, f32[48,64,64]{2,1,0:T(8,128)S(1)}, s32[]{:T(128)}, bf16[32,48]{1,0:T(8,128)(2,1)}, bf16[32,48,64,64]{3,2,1,0:T(8,128)(2,1)}, /*index=5*/s32[]{:T(128)}, s32[]{:T(128)}, s32[]{:T(128)}, s32[]{:T(128)}) while((s32[]{:T(128)}, f32[48,64,64]{2,1,0:T(8,128)S(1)}, s32[]{:T(128)}, bf16[32,48]{1,0:T(8,128)(2,1)}, ...), condition=%wide.region_21.22_spmd, body=%wide.region_20.21_spmd.sunk | while | flops 589878 | bytes 1966715 | solution.py:32
  1298.6 2.4 fusion.13
  1302.2 4.1 fusion.11
  1306.3 2.3 copy.78
  (279 shorter events, 156.0 us)
Async XLA Ops:
  7.2 361.2 %copy-start = (bf16[1,288,3072]{2,1,0:T(8,128)(2,1)S(1)}, bf16[1,288,3072]{2,1,0:T(8,128)(2,1)}, u32[]{:S(2)}) copy-start(bf16[1,288,3072]{2,1,0:T(8,128)(2,1)} %param.33) | copy-start | bytes 5308420
  7.2 194.1 %all-gather.12.cloned.1.call-start = ((), (), s32[]{:S(2)}) async-start(), calls=%async_computation.10 | async-start | bytes 25952256 | tf_op jit(solution)/shard_map/all_gather | solution.py:17
  8.4 77.3 %copy-start.24 = (f32[48,128]{1,0:T(8,128)}, f32[48,128]{1,0:T(8,128)S(1)}, u32[]{:S(2)}) copy-start(f32[48,128]{1,0:T(8,128)S(1)} %reduce_window_sum.22) | copy-start | bytes 73732
  10.2 75.5 %copy-start.2 = (bf16[1,128,3072]{1,2,0:T(8,128)(2,1)}, bf16[1,128,3072]{1,2,0:T(8,128)(2,1)S(1)}, u32[]{:S(2)}) copy-start(bf16[1,128,3072]{1,2,0:T(8,128)(2,1)S(1)} %copy.58) | copy-start | bytes 2359300
  12.0 74.8 %copy-start.4 = (bf16[1,128,3072]{1,2,0:T(8,128)(2,1)}, bf16[1,128,3072]{1,2,0:T(8,128)(2,1)S(1)}, u32[]{:S(2)}) copy-start(bf16[1,128,3072]{1,2,0:T(8,128)(2,1)S(1)} %copy.60) | copy-start | bytes 2359300
  12.0 70.9 %copy-start.49 = (s32[1,4]{1,0:T(1,128)S(1)}, s32[1,4]{1,0:T(1,128)}, u32[]{:S(2)}) copy-start(s32[1,4]{1,0:T(1,128)} %param.24) | copy-start | bytes 52
  12.1 72.5 %copy-start.36 = (bf16[1,4,3072]{2,1,0:T(4,128)(2,1)S(1)}, bf16[1,4,3072]{2,1,0:T(4,128)(2,1)}, u32[]{:S(2)}) copy-start(bf16[1,4,3072]{2,1,0:T(4,128)(2,1)} %param.20) | copy-start | bytes 73732
  12.1 72.6 %copy-start.25 = (bf16[1,4,3072]{2,1,0:T(4,128)(2,1)S(1)}, bf16[1,4,3072]{2,1,0:T(4,128)(2,1)}, u32[]{:S(2)}) copy-start(bf16[1,4,3072]{2,1,0:T(4,128)(2,1)} %param.19) | copy-start | bytes 73732
  14.3 348.2 %all-gather.8.cloned.1.call-start = ((), (), s32[]{:S(2)}) async-start(), calls=%async_computation.6 | async-start | bytes 3244032 | tf_op jit(solution)/shard_map/all_gather | solution.py:71
  84.7 116.8 %copy-start.12 = (bf16[4,48,64]{2,1,0:T(8,128)(2,1)}, bf16[4,48,64]{2,1,0:T(8,128)(2,1)S(1)}, u32[]{:S(2)}) copy-start(bf16[4,48,64]{2,1,0:T(8,128)(2,1)S(1)} %reshape_squeeze.9) | copy-start | bytes 73732
  85.7 115.8 %copy-start.52 = (pred[4,128]{1,0:T(4,128)(4,1)}, pred[4,128]{1,0:T(4,128)(4,1)S(1)}, u32[]{:S(2)}) copy-start(pred[4,128]{1,0:T(4,128)(4,1)S(1)} %iota_compare_fusion.6) | copy-start | bytes 1540
  225.2 364.4 %reduce-scatter.3.cloned.1.call-start = ((), (), s32[]{:S(2)}) async-start(), calls=%async_computation.7 | async-start | bytes 3244032 | tf_op jit(solution)/shard_map/reduce_scatter | solution.py:76
  591.1 14.7 %all-to-all-start.1 = ((bf16[8,2,3072]{2,1,0:T(2,128)(2,1)}), bf16[8,2,3072]{2,1,0:T(2,128)(2,1)}, u32[]{:S(2)}, u32[]{:S(2)}) async-start(bf16[8,2,3072]{2,1,0:T(2,128)(2,1)} %reshape.392), calls=%async_computation.2 | async-start | bytes 196608 | tf_op jit(solution)/shard_map/all_to_all | solution.py:83
  600.8 201.7 %all-gather.10.cloned.1.call-start = ((), (), s32[]{:S(2)}) async-start(), calls=%async_computation.8 | async-start | bytes 3244032 | tf_op jit(solution)/shard_map/all_gather | solution.py:71
  730.9 298.0 %reduce-scatter.5.cloned.1.call-start = ((), (), s32[]{:S(2)}) async-start(), calls=%async_computation.9 | async-start | bytes 3244032 | tf_op jit(solution)/shard_map/reduce_scatter | solution.py:76
  811.4 229.2 %copy-start.45 = (f32[4,1]{0,1:T(1,128)S(1)}, f32[4,1]{0,1:T(1,128)}, u32[]{:S(2)}) copy-start(f32[4,1]{0,1:T(1,128)} %get-tuple-element.175) | copy-start | bytes 52
  811.4 234.3 %copy-start.39 = (bf16[4,2,16]{2,0,1:T(4,128)(2,1)S(1)}, bf16[4,2,16]{2,0,1:T(4,128)(2,1)}, u32[]{:S(2)}) copy-start(bf16[4,2,16]{2,0,1:T(4,128)(2,1)} %copy.67) | copy-start | bytes 772
  811.4 234.5 %copy-start.18 = (f32[4,3072]{1,0:T(4,128)S(1)}, f32[4,3072]{1,0:T(4,128)}, u32[]{:S(2)}) copy-start(f32[4,3072]{1,0:T(4,128)} %reshape.388) | copy-start | bytes 147460
  811.4 234.5 %copy-start.26 = (bf16[1,4,3072]{2,1,0:T(4,128)(2,1)S(1)}, bf16[1,4,3072]{2,1,0:T(4,128)(2,1)}, u32[]{:S(2)}) copy-start(bf16[1,4,3072]{2,1,0:T(4,128)(2,1)} %param.19) | copy-start | bytes 73732
  811.4 234.5 %copy-start.42 = (f32[4]{0:T(128)S(1)}, f32[4]{0:T(128)}, u32[]{:S(2)}) copy-start(f32[4]{0:T(128)} %add_rsqrt_fusion) | copy-start | bytes 52
  812.1 234.9 %copy-start.13 = (bf16[4,48,64]{2,1,0:T(8,128)(2,1)S(1)}, bf16[4,48,64]{2,1,0:T(8,128)(2,1)}, u32[]{:S(2)}) copy-start(bf16[4,48,64]{2,1,0:T(8,128)(2,1)} %copy-done.12) | copy-start | bytes 73732
  1030.5 15.1 %all-to-all-start.3 = ((bf16[8,2,3072]{2,1,0:T(2,128)(2,1)}), bf16[8,2,3072]{2,1,0:T(2,128)(2,1)S(1)}, u32[]{:S(2)}, u32[]{:S(2)}) async-start(bf16[8,2,3072]{2,1,0:T(2,128)(2,1)} %reshape.398), calls=%async_computation.5 | async-start | bytes 196608 | tf_op jit(solution)/shard_map/all_to_all | solution.py:83
  1040.6 189.0 %all-gather.14.cloned.1.call-start = ((), (), s32[]{:S(2)}) async-start(), calls=%async_computation.11 | async-start | bytes 25952256 | tf_op jit(solution)/shard_map/all_gather | solution.py:17
  1229.8 68.9 %copy-start.22 = (f32[128,48]{0,1:T(8,128)S(1)}, f32[128,48]{0,1:T(8,128)}, u32[]{:S(2)}) copy-start(f32[128,48]{0,1:T(8,128)} %copy-done.21) | copy-start | bytes 73732
  (37 other events, 112.2 us)
Sparse Core Ops, SparseCore 0:
  14.5 186.7 all-gather.11
  225.3 137.1 all-gather.7
  372.1 217.4 reduce-scatter.2
  731.0 71.3 all-gather.9
  811.6 217.2 reduce-scatter.4
  1050.3 179.2 all-gather.13
